TPU v7x, 32 devices: a whole 2x2x4 slice. The times are simulated.
32 devices in a mesh: rows: 4 (over z), cols: 8 (over y, x, core).
Axes of the slice: x: 2, y: 2, z: 4, core: 2. Of those that a mesh axis runs over, the one named last changes fastest.
Arguments:
- left_fine: bfloat16 [128, 1024, 128], P('rows', 'cols'), may hold values from -40 to 40
- right_fine: bfloat16 [128, 1024, 128], P('rows', 'cols'), may hold values from -40 to 40
- left_coarse: bfloat16 [32, 256, 128], P('rows', 'cols'), may hold values from -40 to 40
- right_coarse: bfloat16 [32, 256, 128], P('rows', 'cols'), may hold values from -40 to 40
- candidates: int32 [8, 32, 4], P(None, 'rows'), may hold values from 0 to 7, all different within a row; in each aligned block of 8 rows (0 to 7, 8 to 15, ..., all dimensions but the last counted through in order) at most 8 rows name the same one
- counts: int32 [8, 32], P(None, 'rows'), may hold values from 1 to 4
- query_weight: bfloat16 [128, 128], replicated, may hold values from -1 to 1
- key_weight: bfloat16 [128, 128], replicated, may hold values from -1 to 1
- value_weight: bfloat16 [128, 128], replicated, may hold values from -0.5 to 0.5
- out_weight: bfloat16 [128, 128], replicated, may hold values from -0.5 to 0.5
- norm_gain: float32 [128], replicated, may hold values from 0.5 to 1.5
Outputs:
- fine_features: bfloat16 [128, 1024, 128], P('rows', 'cols')
- coarse_prior: bfloat16 [32, 256, 128], P('rows', 'cols')
Inputs may be any that keep to these rules, and one draw needn't show every extreme that they name: `candidates`: each list names 4 different right blocks; entries at k >= counts are not used. For one left block, within the 8 bands of one index of rows (aligned groups of bands), no right block is named more than 8 times, and in some groups one is named exactly 8 times.
All inputs are finite; a program needn't handle non-finite values.
Results may differ from a plain program's by a relative error of at most 0.01.
Values may be sent and summed in bfloat16 or wider, within the bound.
A program may use at most 192 MiB of HBM per device.

v0:
```python
import functools
import math

import jax
import jax.numpy as jnp
import numpy as np
from jax import lax
from jax.experimental import pallas as pl
from jax.experimental.pallas import tpu as pltpu
from jax.sharding import PartitionSpec as P

HEADS = 8
HEAD_DIM = 16
BLOCK = 128
BAND = 4
EPSILON = 1e-05
PAIRS = HEADS // 2
EDGE = 16
EARLY = 3
LEAD = 5
MESH = pl.DeviceIdType.MESH
KEY_SCALE = math.log2(math.e) / math.sqrt(HEAD_DIM)
BF16 = jnp.bfloat16
F32 = jnp.float32


def nt(a, b):
    return lax.dot_general(a, b, (((1,), (1,)), ((), ())), preferred_element_type=F32)


def tn(a, b):
    return lax.dot_general(a, b, (((0,), (0,)), ((), ())), preferred_element_type=F32)


def nn(a, b):
    return jnp.dot(a, b, preferred_element_type=F32)


def layer_norm(values, norm_gain):
    average = jnp.mean(values, axis=-1, keepdims=True)
    centred = values - average
    spread = jnp.mean(centred * centred, axis=-1, keepdims=True)
    return centred * lax.rsqrt(spread + EPSILON) * norm_gain


def upsample_matrix(cols):
    taps = np.array(
        [[0.375, 0.625, 0.0], [0.125, 0.875, 0.0], [0.0, 0.875, 0.125], [0.0, 0.625, 0.375]]
    )
    pitch = cols + 2 * EDGE
    out = np.zeros((BAND, cols, 4, 3, pitch), np.float32)
    for c in range(cols):
        for t in range(4):
            for d in range(3):
                out[:, c, t, :, c + d + EDGE - 1] = taps[:, :] * taps[t, d]
    return out.reshape(BAND * cols * 4, 3 * pitch)


def project_blocks(blocks, wkv_ref):
    feat = blocks[0].shape[1]
    keys, values = [], []
    for block in blocks:
        both = nn(block, wkv_ref[...])
        keys.append((both[:, :feat] * KEY_SCALE).astype(BF16))
        values.append(both[:, feat:].astype(BF16).T)
    return jnp.concatenate(keys, axis=0), jnp.concatenate(values, axis=1)


def attend(keys, values, ones, spread_ref):
    parts = []
    width = spread_ref.shape[1] // HEADS

    def score(pair):
        return nn(keys, spread_ref[:, pair * 2 * width : (pair + 1) * 2 * width])

    ahead = score(0)
    for pair in range(PAIRS):
        scores = ahead
        if pair + 1 < PAIRS:
            ahead = score(pair + 1)
        top = jnp.max(scores, axis=0, keepdims=True)
        weights = jnp.exp2((scores - top).astype(BF16))
        rows = values[pair * 2 * HEAD_DIM : (pair + 1) * 2 * HEAD_DIM]
        mix = nn(jnp.concatenate([rows, ones], axis=0), weights)
        inverse = 1.0 / mix[2 * HEAD_DIM : 2 * HEAD_DIM + 1]
        parts.append(mix[:HEAD_DIM, :width] * inverse[:, :width])
        parts.append(mix[HEAD_DIM : 2 * HEAD_DIM, width:] * inverse[:, width:])
    return jnp.concatenate(parts, axis=0).astype(BF16)


def query_stage(left, coarse, up_ref, wq_ref):
    up = nn(up_ref[...], coarse)
    query_in = (left.reshape(up.shape).astype(F32) + up).astype(BF16)
    return query_in, nt(wq_ref[...], query_in).astype(BF16)


def spread_queries(query_ref, spread_ref, start):
    for h in range(HEADS):
        rows = slice(h * HEAD_DIM, (h + 1) * HEAD_DIM)
        spread_ref[rows, h * BLOCK : (h + 1) * BLOCK] = query_ref[rows, pl.ds(start, BLOCK)]


def out_stage(query_in, mixed, wo_ref, gain_ref):
    product = tn(mixed, wo_ref[...])
    return layer_norm(query_in.astype(F32) + product, gain_ref[...]).astype(BF16)


def flipped(index, bit):
    return index + bit - 2 * bit * ((index // bit) % 2)


def gather_hops(n, me):
    if n != 8:
        return [(me, (me + j) % n, (me + n - j) % n, None) for j in range(1, n)]
    a, b, c = flipped(me, 1), flipped(me, 2), flipped(me, 4)
    d = flipped(b, 4)
    odd = me % 2
    relay_block = b + odd * (c - b)
    relay_target = c + odd * (b - c)
    return [
        (me, b, b, None),
        (me, c, c, None),
        (me, a, a, None),
        (relay_block, relay_target, d, (0, 1)),
        (b, a, flipped(b, 1), (0,)),
        (c, a, flipped(c, 1), (1,)),
        (d, a, flipped(d, 1), (3,)),
    ]


def gather_kernel(
    list_ref,
    count_ref,
    left_ref,
    right_ref,
    left_coarse_ref,
    right_coarse_ref,
    up_ref,
    wq_ref,
    wkv_ref,
    wo_ref,
    gain_ref,
    fold_ref,
    late_ref,
    fine_ref,
    prior_ref,
    ext_ref,
    *scratch,
    n,
    row_devices,
    early,
    length,
):
    bands_ref = scratch[:early]
    (
        coarse_ref,
        edge_low_ref,
        edge_high_ref,
        rows_ref,
        query_ref,
        spread_ref,
        mix_ref,
        coarse_send,
        coarse_recv,
        edge_send,
        edge_recv,
        fine_send,
        fine_recv,
        local_sem,
    ) = scratch[early:]
    me = lax.axis_index("cols")
    row = lax.axis_index("rows")
    bands = right_ref.shape[0] // BAND
    coarse_rows, coarse_cols, feat = left_coarse_ref.shape
    hops = gather_hops(n, me)

    barrier = pltpu.get_barrier_semaphore()
    for j in range(1, n):
        pl.semaphore_signal(
            barrier, inc=1, device_id={"cols": (me + j) % n}, device_id_type=MESH
        )

    @pl.when(row > 0)
    def _():
        pl.semaphore_signal(barrier, inc=1, device_id={"rows": row - 1}, device_id_type=MESH)

    @pl.when(row < row_devices - 1)
    def _():
        pl.semaphore_signal(barrier, inc=1, device_id={"rows": row + 1}, device_id_type=MESH)

    inner = (row > 0).astype(jnp.int32) + (row < row_devices - 1).astype(jnp.int32)
    pl.semaphore_wait(barrier, n - 1 + inner)

    def coarse_copy(j):
        return pltpu.make_async_remote_copy(
            src_ref=right_coarse_ref,
            dst_ref=coarse_ref.at[me],
            send_sem=coarse_send.at[j - 1],
            recv_sem=coarse_recv.at[j - 1],
            device_id={"cols": (me + j) % n},
            device_id_type=MESH,
        )

    def place(g, block):
        if g < early:
            return bands_ref[g].at[block]
        return late_ref.at[block, pl.ds((g - early) * BAND, BAND)]

    def fine_copy(g, hop):
        block, target, _, after = hops[hop]
        if after is None:
            source = right_ref.at[pl.ds(g * BAND, BAND)]
        else:
            source = place(g, block)
        return pltpu.make_async_remote_copy(
            src_ref=source,
            dst_ref=place(g, block),
            send_sem=fine_send.at[g, hop],
            recv_sem=fine_recv.at[g, hop],
            device_id={"cols": target},
            device_id_type=MESH,
        )

    def own_copy(g):
        return pltpu.make_async_copy(
            right_ref.at[pl.ds(g * BAND, BAND)], place(g, me), local_sem.at[g]
        )

    arrived = [set() for _ in range(bands)]

    def take(g, hop):
        if hop not in arrived[g]:
            arrived[g].add(hop)
            fine_copy(g, hop).wait_recv()

    levels = []
    for hop in hops:
        levels.append(0 if hop[3] is None else 1 + max(levels[i] for i in hop[3]))
    depth = max(levels)

    def send(g, level):
        for hop in range(len(hops)):
            if levels[hop] == level:
                for needed in hops[hop][3] or ():
                    take(g, needed)
                fine_copy(g, hop).start()

    ticks = []
    for t in range(1, bands + depth):
        ticks.append(
            [(t - level, level) for level in range(depth, 0, -1) if 0 <= t - level < bands]
            + ([(t + LEAD - 1, 0)] if t + LEAD - 1 < bands else [])
        )

    def tick():
        if ticks:
            for g, level in ticks.pop(0):
                send(g, level)

    for j in range(1, n):
        coarse_copy(j).start()
    for g in range(bands):
        own_copy(g).start()
    for g in range(min(LEAD, bands)):
        send(g, 0)

    spread_ref[...] = jnp.zeros_like(spread_ref)
    coarse_ref[me] = right_coarse_ref[...]
    for j in range(1, n):
        coarse_copy(j).wait()

    wide = HEADS * coarse_cols
    diagonal = (
        lax.broadcasted_iota(jnp.int32, (feat, wide), 0) // HEAD_DIM
        == lax.broadcasted_iota(jnp.int32, (feat, wide), 1) // coarse_cols
    )

    def coarse_row(r, carry):
        right = coarse_ref[:, r].reshape(n * coarse_cols, feat)
        left = left_coarse_ref[r]
        keys, values = project_blocks([right], wkv_ref)
        queries = nt(wq_ref[...], jnp.concatenate([left] * HEADS, axis=0))
        queries = jnp.where(diagonal, queries, 0.0).astype(BF16)
        scores = nn(keys, queries)
        top = jnp.max(scores, axis=0, keepdims=True)
        weights = jnp.exp2((scores - top).astype(BF16))
        total = jnp.sum(weights.astype(F32), axis=0, keepdims=True)
        mixed = nn(values, weights) * (1.0 / total)
        mixed = jnp.where(diagonal, mixed, 0.0).astype(BF16)
        folded = nt(fold_ref[...], mixed).astype(BF16)
        out = left.astype(F32) + nn(folded, wo_ref[...])
        out = layer_norm(out, gain_ref[...]).astype(BF16)
        rows_ref[r + 1] = out
        prior_ref[r] = out
        return carry

    lax.fori_loop(0, coarse_rows // 2, coarse_row, 0)
    tick()
    lax.fori_loop(coarse_rows // 2, coarse_rows, coarse_row, 0)

    def row_copy(up):
        return pltpu.make_async_remote_copy(
            src_ref=prior_ref.at[0 if up else coarse_rows - 1],
            dst_ref=rows_ref.at[coarse_rows + 1 if up else 0],
            send_sem=edge_send.at[0 if up else 1],
            recv_sem=edge_recv.at[0 if up else 1],
            device_id={"rows": row - 1 if up else row + 1},
            device_id_type=MESH,
        )

    def col_copy(left):
        return pltpu.make_async_remote_copy(
            src_ref=rows_ref.at[:, pl.ds(0 if left else coarse_cols - EDGE, EDGE)],
            dst_ref=edge_high_ref if left else edge_low_ref,
            send_sem=edge_send.at[2 if left else 3],
            recv_sem=edge_recv.at[2 if left else 3],
            device_id={"cols": me - 1 if left else me + 1},
            device_id_type=MESH,
        )

    has = (row > 0, row < row_devices - 1, me > 0, me < n - 1)

    @pl.when(has[0])
    def _():
        row_copy(True).start()

    @pl.when(has[1])
    def _():
        row_copy(False).start()

    @pl.when(has[0])
    def _():
        row_copy(False).wait_recv()
        row_copy(True).wait_send()

    @pl.when(jnp.logical_not(has[0]))
    def _():
        rows_ref[0] = rows_ref[1]

    @pl.when(has[1])
    def _():
        row_copy(True).wait_recv()
        row_copy(False).wait_send()

    @pl.when(jnp.logical_not(has[1]))
    def _():
        rows_ref[coarse_rows + 1] = rows_ref[coarse_rows]

    @pl.when(has[2])
    def _():
        col_copy(True).start()

    @pl.when(has[3])
    def _():
        col_copy(False).start()

    tick()

    @pl.when(has[2])
    def _():
        col_copy(False).wait_recv()
        col_copy(True).wait_send()

    @pl.when(jnp.logical_not(has[2]))
    def _():
        edge_low_ref[...] = jnp.broadcast_to(rows_ref[:, 0:1], edge_low_ref.shape)

    @pl.when(has[3])
    def _():
        col_copy(True).wait_recv()
        col_copy(False).wait_send()

    @pl.when(jnp.logical_not(has[3]))
    def _():
        edge_high_ref[...] = jnp.broadcast_to(
            rows_ref[:, coarse_cols - 1 : coarse_cols], edge_high_ref.shape
        )

    ext_ref[:, :EDGE] = edge_low_ref[...]
    ext_ref[:, EDGE : EDGE + coarse_cols] = rows_ref[...]
    ext_ref[:, EDGE + coarse_cols :] = edge_high_ref[...]

    for g in range(early):
        tick()
        own_copy(g).wait()
        for hop in range(len(hops)):
            take(g, hop)
        coarse = jnp.concatenate([ext_ref[g + i] for i in range(3)], axis=0)
        query_in, queries = query_stage(left_ref[g * BAND : (g + 1) * BAND], coarse, up_ref, wq_ref)
        query_ref[...] = queries
        used = count_ref[g]
        picks = [
            jnp.where(k < used, list_ref[g * length + k], list_ref[g * length])
            for k in range(length)
        ]
        lanes = lax.broadcasted_iota(jnp.int32, (1, length * BLOCK), 1)
        live = jnp.where(lanes < used * BLOCK, 1.0, 0.0).astype(BF16)

        def fine_row(r, carry, g=g, picks=picks, live=live):
            keys, values = project_blocks(
                [bands_ref[g][picks[k], r] for k in range(length)], wkv_ref
            )
            values = values * live
            ones = jnp.broadcast_to(live, (HEAD_DIM, live.shape[1]))
            start = pl.multiple_of(r * BLOCK, BLOCK)
            spread_queries(query_ref, spread_ref, start)
            mix_ref[:, pl.ds(start, BLOCK)] = attend(keys, values, ones, spread_ref)
            return carry

        lax.fori_loop(0, BAND // 2, fine_row, 0)
        tick()
        if g > 0:
            tick()
        lax.fori_loop(BAND // 2, BAND, fine_row, 0)
        out = out_stage(query_in, mix_ref[...], wo_ref, gain_ref)
        fine_ref[g * BAND : (g + 1) * BAND] = out.reshape(BAND, BLOCK, feat)

    while ticks:
        tick()
    for g in range(bands):
        if g >= early:
            own_copy(g).wait()
        for hop in range(len(hops)):
            take(g, hop)
            fine_copy(g, hop).wait_send()


def gather_stage(mesh_rows, n, left_fine, right_fine, left_coarse, right_coarse, lists, counts, w):
    rows, cols, feat = left_fine.shape
    bands = rows // BAND
    early = min(EARLY, bands - 1)
    coarse_rows, coarse_cols, _ = left_coarse.shape
    fold = np.tile(np.eye(coarse_cols, dtype=np.float32), (1, HEADS))
    hop_count = len(gather_hops(n, 0))
    vmem = pl.BlockSpec(memory_space=pltpu.VMEM)
    smem = pl.BlockSpec(memory_space=pltpu.SMEM)
    return pl.pallas_call(
        functools.partial(
            gather_kernel, n=n, row_devices=mesh_rows, early=early, length=lists.shape[1]
        ),
        out_shape=(
            jax.ShapeDtypeStruct((n, (bands - early) * BAND, cols, feat), BF16),
            jax.ShapeDtypeStruct((early * BAND, cols, feat), BF16),
            jax.ShapeDtypeStruct(left_coarse.shape, BF16),
            jax.ShapeDtypeStruct((coarse_rows + 2, coarse_cols + 2 * EDGE, feat), BF16),
        ),
        in_specs=[smem, smem] + [vmem] * 10,
        out_specs=(pl.BlockSpec(memory_space=pl.ANY), vmem, vmem, vmem),
        scratch_shapes=[pltpu.VMEM((n, BAND, cols, feat), BF16) for _ in range(early)]
        + [
            pltpu.VMEM((n,) + right_coarse.shape, BF16),
            pltpu.VMEM((coarse_rows + 2, EDGE, feat), BF16),
            pltpu.VMEM((coarse_rows + 2, EDGE, feat), BF16),
            pltpu.VMEM((coarse_rows + 2, coarse_cols, feat), BF16),
            pltpu.VMEM((feat, BAND * BLOCK), BF16),
            pltpu.VMEM((feat, HEADS * BLOCK), BF16),
            pltpu.VMEM((feat, BAND * BLOCK), BF16),
            pltpu.SemaphoreType.DMA((n - 1,)),
            pltpu.SemaphoreType.DMA((n - 1,)),
            pltpu.SemaphoreType.DMA((4,)),
            pltpu.SemaphoreType.DMA((4,)),
            pltpu.SemaphoreType.DMA((bands, hop_count)),
            pltpu.SemaphoreType.DMA((bands, hop_count)),
            pltpu.SemaphoreType.DMA((bands,)),
        ],
        compiler_params=pltpu.CompilerParams(collective_id=0, has_side_effects=True),
        name="gather_stage",
    )(
        lists.reshape(-1),
        counts,
        left_fine,
        right_fine,
        left_coarse,
        right_coarse,
        w["up"],
        w["wq"],
        w["wkv"],
        w["wo"],
        w["gain"],
        jnp.asarray(fold, BF16),
    )


def fine_kernel(
    list_ref,
    count_ref,
    left_ref,
    ext_ref,
    up_ref,
    wq_ref,
    wkv_ref,
    wo_ref,
    gain_ref,
    done_ref,
    *refs,
    early,
):
    list_length = len(refs) - 4
    cand_refs = refs[:list_length]
    out_ref, query_ref, spread_ref, mix_ref = refs[list_length:]
    band = pl.program_id(0)
    feat = wq_ref.shape[0]

    @pl.when(pl.program_id(0) == 0)
    def _():
        spread_ref[...] = jnp.zeros_like(spread_ref)

    @pl.when(band < early)
    def _():
        out_ref[...] = done_ref[...]

    @pl.when(band >= early)
    def _():
        coarse = jnp.concatenate([ext_ref[band + i] for i in range(3)], axis=0)
        query_in, queries = query_stage(left_ref[...], coarse, up_ref, wq_ref)
        query_ref[...] = queries

        for used in range(1, list_length + 1):

            @pl.when(count_ref[band] == used)
            def _():
                def row(r, carry):
                    keys, values = project_blocks(
                        [cand_refs[k][0, r] for k in range(used)], wkv_ref
                    )
                    ones = jnp.ones((HEAD_DIM, used * BLOCK), BF16)
                    start = pl.multiple_of(r * BLOCK, BLOCK)
                    spread_queries(query_ref, spread_ref, start)
                    mix_ref[:, pl.ds(start, BLOCK)] = attend(keys, values, ones, spread_ref)
                    return carry

                lax.fori_loop(0, BAND, row, 0)

        out_ref[...] = out_stage(query_in, mix_ref[...], wo_ref, gain_ref).reshape(out_ref.shape)


def fine_stage(left_fine, gathered, done, ext, lists, counts, w):
    rows, cols, feat = left_fine.shape
    bands = rows // BAND
    early = bands - gathered.shape[1] // BAND
    length = lists.shape[1]

    def whole(shape):
        return pl.BlockSpec(shape, lambda g, c, n: (0,) * len(shape))

    def picked(k):
        return pl.BlockSpec(
            (1, BAND, cols, feat),
            lambda g, c, n: (c[jnp.maximum(g, early) * length + k], jnp.maximum(g - early, 0), 0, 0),
        )

    def banded(index):
        return pl.BlockSpec((BAND, cols, feat), lambda g, c, n: (index(g), 0, 0))

    names = ("up", "wq", "wkv", "wo", "gain")
    return pl.pallas_call(
        functools.partial(fine_kernel, early=early),
        grid_spec=pltpu.PrefetchScalarGridSpec(
            num_scalar_prefetch=2,
            grid=(bands,),
            in_specs=[banded(lambda g: jnp.maximum(g, early)), whole(ext.shape)]
            + [whole(w[name].shape) for name in names]
            + [banded(lambda g: jnp.minimum(g, early - 1))]
            + [picked(k) for k in range(length)],
            out_specs=banded(lambda g: g),
            scratch_shapes=[
                pltpu.VMEM((feat, BAND * BLOCK), BF16),
                pltpu.VMEM((feat, HEADS * BLOCK), BF16),
                pltpu.VMEM((feat, BAND * BLOCK), BF16),
            ],
        ),
        out_shape=jax.ShapeDtypeStruct(left_fine.shape, BF16),
        name="fine_stage",
    )(
        lists.reshape(-1),
        counts,
        left_fine,
        ext,
        *[w[name] for name in names],
        done,
        *([gathered] * length),
    )


def body(
    left_fine,
    right_fine,
    left_coarse,
    right_coarse,
    candidates,
    counts,
    query_weight,
    key_weight,
    value_weight,
    out_weight,
    norm_gain,
):
    me = lax.axis_index("cols")
    lists = lax.dynamic_index_in_dim(candidates, me, 0, keepdims=False)
    own_counts = lax.dynamic_index_in_dim(counts, me, 0, keepdims=False)
    w = {
        "up": jnp.asarray(upsample_matrix(left_coarse.shape[1]), BF16),
        "wq": query_weight.T,
        "wkv": jnp.concatenate([key_weight, value_weight], axis=1),
        "wo": out_weight,
        "gain": norm_gain.reshape(1, -1),
    }
    gathered, done, coarse_prior, ext = gather_stage(
        lax.axis_size("rows"),
        lax.axis_size("cols"),
        left_fine,
        right_fine,
        left_coarse,
        right_coarse,
        lists,
        own_counts,
        w,
    )
    fine_features = fine_stage(left_fine, gathered, done, ext, lists, own_counts, w)
    return (fine_features, coarse_prior)


def solution(mesh):
    return jax.shard_map(
        body,
        mesh=mesh,
        in_specs=(
            P("rows", "cols", None),
            P("rows", "cols", None),
            P("rows", "cols", None),
            P("rows", "cols", None),
            P(None, "rows", None),
            P(None, "rows"),
            P(),
            P(),
            P(),
            P(),
            P(),
        ),
        out_specs=(P("rows", "cols", None), P("rows", "cols", None)),
        check_vma=False,
    )
```

profile of v0, /device:TPU:1, one launch (start us, length us, event | category | flops | bytes accessed | tf_op | source)
XLA Modules:
  0.0 100.8 jit_solution(8645745054030957492)
XLA Ops:
  0.6 0.0 copy-start
  0.6 1.2 %dynamic-slice_bitcast_fusion.count_ref = s32[8]{0:T(128)} fusion(s32[8,8]{1,0:T(8,128)} %param.18, s32[]{:T(128)S(6)} %select_n.6), kind=kLoop, calls=%fused_computation.2 | loop fusion | bytes 68 | tf_op jit(solution)/shard_map/jit(dynamic_index_in_dim)/squeeze | solution.py:600
  1.9 0.0 copy-done
  1.9 0.1 copy.17
  2.0 0.7 reshape.12.list_ref
  2.6 1.5 %copy.18 = bf16[128,128]{0,1:T(8,128)(2,1)} copy(bf16[128,128]{1,0:T(8,128)(2,1)} %param.19) | data formatting | bytes 65536 | tf_op args[6]
  4.1 0.8 constant_dynamic-update-slice_fusion.1
  4.9 0.8 constant_dynamic-update-slice_fusion.wkv_ref
  5.6 0.0 copy-start.1
  5.6 0.6 copy-done.1
  6.3 64.1 %gather_stage.1 = (bf16[8,20,128,128]{3,2,1,0:T(8,128)(2,1)}, bf16[12,128,128]{2,1,0:T(8,128)(2,1)}, bf16[8,32,128]{2,1,0:T(8,128)(2,1)}, bf16[10,64,128]{2,1,0:T(8,128)(2,1)}) custom-call(s32[32]{0:T(128)} %reshape.12.list_ref, s32[8]{0:T(128)} %dynamic-slice_bitcast_fusion.count_ref, bf16[32,128,128]{2,1,0:T(8,128)(2,1)} %left_ref.3, ...), custom_call_target="tpu_custom_call" | custom-call | tf_op jit(solution)/shard_map/gather_stage/pallas_call | solution.py:437
  70.3 0.0 copy-start.2
  70.3 29.9 %fine_stage.1 = bf16[32,128,128]{2,1,0:T(8,128)(2,1)} custom-call(s32[32]{0:T(128)} %reshape.12.list_ref, s32[8]{0:T(128)} %dynamic-slice_bitcast_fusion.count_ref, bf16[32,128,128]{2,1,0:T(8,128)(2,1)} %left_ref.3, bf16[10,64,128]{2,1,0:T(8,128)(2,1)} %get-tuple-element.6.ext_ref, bf16[512,192]{1,0:T(8,128)(2,1)} %constant.18.clone.up_ref, ...), custom_call_target="tpu_custom_call" | custom-call | tf_op jit(solution)/shard_map/fine_stage/pallas_call | solution.py:556
  100.2 0.0 copy-done.2
  100.2 0.6 copy.21
  (1 shorter events, 0.0 us)
Async XLA Ops:
  0.6 1.2 %copy-start = (s32[8,8,4]{1,2,0:T(4,128)S(1)}, s32[8,8,4]{1,2,0:T(4,128)}, u32[]{:S(2)}) copy-start(s32[8,8,4]{1,2,0:T(4,128)} %param.17) | copy-start | bytes 3076
  5.6 0.6 copy-start.1
  70.3 29.9 %copy-start.2 = (bf16[8,32,128]{2,1,0:T(8,128)(2,1)S(1)}, bf16[8,32,128]{2,1,0:T(8,128)(2,1)}, u32[]{:S(2)}) copy-start(bf16[8,32,128]{2,1,0:T(8,128)(2,1)} %get-tuple-element.13) | copy-start | bytes 196612
where the time goes:
time: 103 us; the launch traced here: 101 us
  Pallas kernels  93.9 us (91%)
  local copies, waits for them, and re-layouts  6.24 us (6%)
    pallas_call x1, Pallas kernels, gather_stage(): pl.pallas_call(functools.partial(gather_kernel, n=n, row_devices=mesh_row...  64.1 us
    pallas_call x1, Pallas kernels, fine_stage(): pl.pallas_call(functools.partial(fine_kernel, early=early), grid_spec=plt...  29.9 us
    unnamed x9, local copies, waits for them, and re-layouts  3.5 us

commit v1 on v0

--- a/solution.py
+++ b/solution.py
@@ -16,8 +16,8 @@
 EPSILON = 1e-05
 PAIRS = HEADS // 2
 EDGE = 16
-EARLY = 3
-LEAD = 5
+EARLY = 6
+LEAD = 4
 MESH = pl.DeviceIdType.MESH
 KEY_SCALE = math.log2(math.e) / math.sqrt(HEAD_DIM)
 BF16 = jnp.bfloat16
@@ -381,7 +381,8 @@
     ext_ref[:, EDGE + coarse_cols :] = edge_high_ref[...]
 
     for g in range(early):
-        tick()
+        if g == 0:
+            tick()
         own_copy(g).wait()
         for hop in range(len(hops)):
             take(g, hop)
@@ -409,8 +410,6 @@
 
         lax.fori_loop(0, BAND // 2, fine_row, 0)
         tick()
-        if g > 0:
-            tick()
         lax.fori_loop(BAND // 2, BAND, fine_row, 0)
         out = out_stage(query_in, mix_ref[...], wo_ref, gain_ref)
         fine_ref[g * BAND : (g + 1) * BAND] = out.reshape(BAND, BLOCK, feat)

time: 103 us -> 94.3 us (0.916)
  Pallas kernels: 93.9 us -> 86.2 us
    pallas_call x1, Pallas kernels: 29.9 us -> 16 us  [fine_stage(): pl.pallas_call(functools.partial(fine_kernel, early=early), grid_spec=plt...]
    pallas_call x1, Pallas kernels: 64.1 us -> 70.2 us  [gather_stage(): pl.pallas_call(functools.partial(gather_kernel, n=n, row_devices=mesh_row...]
where the time goes in v1:
time: 94.3 us; the launch traced here: 93.1 us
  Pallas kernels  86.2 us (91%)
  local copies, waits for them, and re-layouts  6.19 us (7%)
    pallas_call x1, Pallas kernels, gather_stage(): pl.pallas_call(functools.partial(gather_kernel, n=n, row_devices=mesh_row...  70.2 us
    pallas_call x1, Pallas kernels, fine_stage(): pl.pallas_call(functools.partial(fine_kernel, early=early), grid_spec=plt...  16 us
    unnamed x9, local copies, waits for them, and re-layouts  3.5 us

profile of v1, /device:TPU:1, one launch (start us, length us, event | category | flops | bytes accessed | tf_op | source)
XLA Modules:
  0.0 93.1 jit_solution(6417685429535931118)
XLA Ops:
  0.6 0.0 copy-start
  0.6 1.3 %dynamic-slice_bitcast_fusion.count_ref = s32[8]{0:T(128)} fusion(s32[8,8]{1,0:T(8,128)} %param.18, s32[]{:T(128)S(6)} %select_n.6), kind=kLoop, calls=%fused_computation.2 | loop fusion | bytes 68 | tf_op jit(solution)/shard_map/jit(dynamic_index_in_dim)/squeeze | solution.py:599
  1.9 0.0 copy-done
  1.9 0.1 copy.17
  2.0 0.6 reshape.12.list_ref
  2.6 1.5 %copy.18 = bf16[128,128]{0,1:T(8,128)(2,1)} copy(bf16[128,128]{1,0:T(8,128)(2,1)} %param.19) | data formatting | bytes 65536 | tf_op args[6]
  4.0 0.8 constant_dynamic-update-slice_fusion.1
  4.8 0.8 constant_dynamic-update-slice_fusion.wkv_ref
  5.6 0.0 copy-start.1
  5.6 0.6 copy-done.1
  6.2 70.2 %gather_stage.1 = (bf16[8,8,128,128]{3,2,1,0:T(8,128)(2,1)}, bf16[24,128,128]{2,1,0:T(8,128)(2,1)}, bf16[8,32,128]{2,1,0:T(8,128)(2,1)}, bf16[10,64,128]{2,1,0:T(8,128)(2,1)}) custom-call(s32[32]{0:T(128)} %reshape.12.list_ref, s32[8]{0:T(128)} %dynamic-slice_bitcast_fusion.count_ref, bf16[32,128,128]{2,1,0:T(8,128)(2,1)} %left_ref.3, ...), custom_call_target="tpu_custom_call" | custom-call | tf_op jit(solution)/shard_map/gather_stage/pallas_call | solution.py:436
  76.4 0.0 copy-start.2
  76.4 16.0 %fine_stage.1 = bf16[32,128,128]{2,1,0:T(8,128)(2,1)} custom-call(s32[32]{0:T(128)} %reshape.12.list_ref, s32[8]{0:T(128)} %dynamic-slice_bitcast_fusion.count_ref, bf16[32,128,128]{2,1,0:T(8,128)(2,1)} %left_ref.3, bf16[10,64,128]{2,1,0:T(8,128)(2,1)} %get-tuple-element.6.ext_ref, bf16[512,192]{1,0:T(8,128)(2,1)} %constant.18.clone.up_ref, ...), custom_call_target="tpu_custom_call" | custom-call | tf_op jit(solution)/shard_map/fine_stage/pallas_call | solution.py:555
  92.4 0.0 copy-done.2
  92.4 0.6 copy.21
  (1 shorter events, 0.0 us)
Async XLA Ops:
  0.6 1.3 %copy-start = (s32[8,8,4]{1,2,0:T(4,128)S(1)}, s32[8,8,4]{1,2,0:T(4,128)}, u32[]{:S(2)}) copy-start(s32[8,8,4]{1,2,0:T(4,128)} %param.17) | copy-start | bytes 3076
  5.6 0.6 copy-start.1
  76.4 16.0 %copy-start.2 = (bf16[8,32,128]{2,1,0:T(8,128)(2,1)S(1)}, bf16[8,32,128]{2,1,0:T(8,128)(2,1)}, u32[]{:S(2)}) copy-start(bf16[8,32,128]{2,1,0:T(8,128)(2,1)} %get-tuple-element.13) | copy-start | bytes 196612
